TPU v7x, 32 devices: a whole 2x2x4 slice. The times are simulated.
32 devices in a mesh: dp: 8 (over y, x, core), tensor: 4 (over z).
Axes of the slice: x: 2, y: 2, z: 4, core: 2. Of those that a mesh axis runs over, the one named last changes fastest.
Arguments:
- tokens: bfloat16 [16384, 768], P('dp'), may hold values from -24 to 24
- lengths: int32 [8, 8], P('dp'), may hold values from 1 to 512, 2048 in all within a row
- w_qkv: bfloat16 [3, 768, 768], P(None, None, 'tensor'), may hold values from -0.21875 to 0.21875
- b_qv: bfloat16 [2, 768], P(None, 'tensor'), may hold values from -3 to 3
- w_out: bfloat16 [768, 768], P('tensor'), may hold values from -0.875 to 0.875
- b_out: bfloat16 [768], replicated, may hold values from -3 to 3
- ln1_gain: bfloat16 [768], replicated, may hold values from 0.099609375 to 1.8984375
- ln1_bias: bfloat16 [768], replicated, may hold values from -3 to 3
- w_up: bfloat16 [768, 3072], P(None, 'tensor'), may hold values from -0.21875 to 0.21875
- b_up: bfloat16 [3072], P('tensor'), may hold values from -3 to 3
- w_down: bfloat16 [3072, 768], P('tensor'), may hold values from -0.109375 to 0.109375
- b_down: bfloat16 [768], replicated, may hold values from -3 to 3
- ln2_gain: bfloat16 [768], replicated, may hold values from 0.099609375 to 1.8984375
- ln2_bias: bfloat16 [768], replicated, may hold values from -3 to 3
- cotangent: bfloat16 [16384, 768], P('dp'), may hold values from -24 to 24
Outputs:
- layer_out: bfloat16 [16384, 768], P(('dp', 'tensor'))
- input_grad: bfloat16 [16384, 768], P(('dp', 'tensor'))
- grad_qkv: float32 [3, 768, 768], P(None, 'dp', 'tensor')
- grad_qv_bias: float32 [2, 768], P(None, 'tensor')
- grad_out: float32 [768, 768], P('tensor', 'dp')
- grad_out_bias: float32 [768], P('dp')
- grad_norm1_gain: float32 [768], P('dp')
- grad_norm1_bias: float32 [768], P('dp')
- grad_up: float32 [768, 3072], P('dp', 'tensor')
- grad_up_bias: float32 [3072], P('tensor')
- grad_down: float32 [3072, 768], P('tensor', 'dp')
- grad_down_bias: float32 [768], P('dp')
- grad_norm2_gain: float32 [768], P('dp')
- grad_norm2_bias: float32 [768], P('dp')
Inputs may be any that keep to these rules, and one draw needn't show every extreme that they name: Each row holds 8 lengths that sum to 2048; the longest pair of every pack has exactly 512 tokens.
All inputs are finite; a program needn't handle non-finite values.
Results may differ from a plain program's by a relative error of at most 0.02.
Values may be sent and summed in bfloat16 or wider, within the bound.
A program may use at most 192 MiB of HBM per device.

v0:
```python
import jax
import jax.numpy as jnp
from jax import lax
from jax.sharding import PartitionSpec as P

HD = 64
MOST = 512
epsilon = 1e-05


def segment_ids(pair_lengths, count):
    pair_ends = jnp.cumsum(pair_lengths)
    positions = jnp.arange(count, dtype=jnp.int32)
    return jnp.sum((positions[:, None] >= pair_ends[None, :]).astype(jnp.int32), axis=1)


def norm_forward(values, gain, shift_bias):
    average = jnp.mean(values, axis=-1, keepdims=True)
    centred = values - average
    inv_spread = lax.rsqrt(jnp.mean(centred * centred, axis=-1, keepdims=True) + epsilon)
    normed = centred * inv_spread
    return (normed * gain + shift_bias, normed, inv_spread)


def norm_backward(upstream, normed, inv_spread, gain):
    scaled = upstream * gain
    adjusted = (
        scaled
        - jnp.mean(scaled, axis=-1, keepdims=True)
        - normed * jnp.mean(scaled * normed, axis=-1, keepdims=True)
    )
    return (adjusted * inv_spread, jnp.sum(upstream * normed, axis=0), jnp.sum(upstream, axis=0))


def gelu_exact(value):
    return jax.nn.gelu(value, approximate=False)


def per_device(
    tokens,
    lengths,
    w_qkv,
    b_qv,
    w_out,
    b_out,
    ln1_gain,
    ln1_bias,
    w_up,
    b_up,
    w_down,
    b_down,
    ln2_gain,
    ln2_bias,
    cotangent,
):
    rows = tokens.shape[0]
    local_width = w_out.shape[0]
    local_heads = local_width // HD
    blocks = rows // MOST
    window_rows = 3 * MOST
    factor = HD ** (-0.5)
    segment = segment_ids(lengths[0], rows)
    segment_pad = jnp.pad(segment, (MOST, MOST), constant_values=-1)
    projected = jnp.einsum("td,cde->cte", tokens, w_qkv, preferred_element_type=jnp.float32)
    bias_rows = jnp.stack([b_qv[0], jnp.zeros_like(b_qv[0]), b_qv[1]]).astype(jnp.float32)
    qkv_low = (projected + bias_rows[:, None, :]).astype(jnp.bfloat16)
    padded = jnp.pad(qkv_low[1:], ((0, 0), (MOST, MOST), (0, 0)))

    def block_scores(block_index):
        offset = block_index * MOST
        queries = lax.dynamic_slice_in_dim(qkv_low[0], offset, MOST, 0).reshape(
            MOST, local_heads, HD
        )
        window = lax.dynamic_slice_in_dim(padded, offset, window_rows, 1).reshape(
            2, window_rows, local_heads, HD
        )
        query_segment = lax.dynamic_slice_in_dim(segment, offset, MOST, 0)
        key_segment = lax.dynamic_slice_in_dim(segment_pad, offset, window_rows, 0)
        allowed = query_segment[:, None] == key_segment[None, :]
        products = (
            jnp.einsum("qhd,khd->hqk", queries, window[0], preferred_element_type=jnp.float32)
            * factor
        )
        return (jnp.where(allowed[None], products, -1e30), queries, window)

    def forward_block(block_index):
        scores, queries, window = block_scores(block_index)
        row_top = jnp.max(scores, axis=-1, keepdims=True)
        row_total = jnp.sum(jnp.exp(scores - row_top), axis=-1, keepdims=True)
        log_total = row_top + jnp.log(row_total)
        soft_weights = jnp.exp(scores - log_total).astype(jnp.bfloat16)
        context = jnp.einsum(
            "hqk,khd->qhd", soft_weights, window[1], preferred_element_type=jnp.float32
        )
        return (context.reshape(MOST, local_width).astype(jnp.bfloat16), log_total[..., 0])

    contexts, log_totals = lax.map(forward_block, jnp.arange(blocks, dtype=jnp.int32))
    context = contexts.reshape(rows, local_width)
    attended = lax.psum(
        jnp.dot(context, w_out, preferred_element_type=jnp.float32).astype(jnp.bfloat16), "tensor"
    ).astype(jnp.float32)
    mixed_one = tokens.astype(jnp.float32) + attended + b_out.astype(jnp.float32)
    gain_one = ln1_gain.astype(jnp.float32)
    hidden_one, normed_one, spread_one = norm_forward(
        mixed_one, gain_one, ln1_bias.astype(jnp.float32)
    )
    hidden_low = hidden_one.astype(jnp.bfloat16)
    pre_act = jnp.dot(hidden_low, w_up, preferred_element_type=jnp.float32) + b_up.astype(
        jnp.float32
    )
    activated = gelu_exact(pre_act).astype(jnp.bfloat16)
    fed = lax.psum(
        jnp.dot(activated, w_down, preferred_element_type=jnp.float32).astype(jnp.bfloat16),
        "tensor",
    ).astype(jnp.float32)
    mixed_two = hidden_one + fed + b_down.astype(jnp.float32)
    gain_two = ln2_gain.astype(jnp.float32)
    output_full, normed_two, spread_two = norm_forward(
        mixed_two, gain_two, ln2_bias.astype(jnp.float32)
    )
    share = rows // lax.axis_size("tensor")
    own_start = lax.axis_index("tensor") * share
    layer_out = lax.dynamic_slice_in_dim(output_full, own_start, share, 0).astype(jnp.bfloat16)
    upstream = cotangent.astype(jnp.float32)
    grad_mixed_two, grad_gain_two, grad_bias_two = norm_backward(
        upstream, normed_two, spread_two, gain_two
    )
    grad_fed = grad_mixed_two.astype(jnp.bfloat16)
    grad_down_t = jnp.einsum("td,tf->df", grad_fed, activated, preferred_element_type=jnp.float32)
    grad_act = jnp.einsum("td,fd->tf", grad_fed, w_down, preferred_element_type=jnp.float32)
    act_pull = jax.vjp(gelu_exact, pre_act)[1]
    grad_pre = act_pull(grad_act)[0].astype(jnp.bfloat16)
    grad_up_local = jnp.einsum(
        "td,tf->df", hidden_low, grad_pre, preferred_element_type=jnp.float32
    )
    up_bias_sum = jnp.sum(grad_pre.astype(jnp.float32), axis=0)
    partial_hidden = jnp.einsum("tf,df->td", grad_pre, w_up, preferred_element_type=jnp.float32)
    grad_hidden_one = (
        lax.psum(partial_hidden.astype(jnp.bfloat16), "tensor").astype(jnp.float32) + grad_mixed_two
    )
    grad_mixed_one, grad_gain_one, grad_bias_one = norm_backward(
        grad_hidden_one, normed_one, spread_one, gain_one
    )
    sum_mixed_one = jnp.sum(grad_mixed_one, axis=0)
    grad_attended = grad_mixed_one.astype(jnp.bfloat16)
    own_mixed_one = lax.dynamic_slice_in_dim(grad_mixed_one, own_start, share, 0)
    grad_out_t = jnp.einsum("td,tc->dc", grad_attended, context, preferred_element_type=jnp.float32)
    grad_context = jnp.einsum(
        "td,cd->tc", grad_attended, w_out, preferred_element_type=jnp.float32
    ).astype(jnp.bfloat16)

    def backward_block(gathered_grads, block_index):
        offset = block_index * MOST
        scores, queries, window = block_scores(block_index)
        soft_weights = jnp.exp(scores - log_totals[block_index][..., None])
        upstream_block = lax.dynamic_slice_in_dim(grad_context, offset, MOST, 0).reshape(
            MOST, local_heads, HD
        )
        grad_values = jnp.einsum(
            "hqk,qhd->khd",
            soft_weights.astype(jnp.bfloat16),
            upstream_block,
            preferred_element_type=jnp.float32,
        )
        grad_weights = jnp.einsum(
            "qhd,khd->hqk", upstream_block, window[1], preferred_element_type=jnp.float32
        )
        row_shift = jnp.sum(grad_weights * soft_weights, axis=-1, keepdims=True)
        grad_scores = (soft_weights * (grad_weights - row_shift)).astype(jnp.bfloat16)
        grad_queries = (
            jnp.einsum("hqk,khd->qhd", grad_scores, window[0], preferred_element_type=jnp.float32)
            * factor
        )
        grad_keys = (
            jnp.einsum("hqk,qhd->khd", grad_scores, queries, preferred_element_type=jnp.float32)
            * factor
        )
        update = jnp.stack(
            [
                grad_keys.reshape(window_rows, local_width),
                grad_values.reshape(window_rows, local_width),
            ]
        )
        current = lax.dynamic_slice_in_dim(gathered_grads, offset, window_rows, 1)
        gathered_grads = lax.dynamic_update_slice_in_dim(
            gathered_grads, current + update, offset, 1
        )
        return (gathered_grads, grad_queries.reshape(MOST, local_width))

    start_grads = jnp.zeros((2, rows + 2 * MOST, local_width), jnp.float32)
    key_value_grads, query_grads = lax.scan(
        backward_block, start_grads, jnp.arange(blocks, dtype=jnp.int32)
    )
    key_value_grads = key_value_grads[:, MOST : MOST + rows]
    grad_qkv_low = jnp.stack(
        [query_grads.reshape(rows, local_width), key_value_grads[0], key_value_grads[1]]
    ).astype(jnp.bfloat16)
    grad_qkv_t = jnp.einsum("td,cte->dce", tokens, grad_qkv_low, preferred_element_type=jnp.float32)
    qkv_bias_sums = jnp.sum(grad_qkv_low.astype(jnp.float32), axis=1)
    partial_input = jnp.einsum(
        "cte,cde->td", grad_qkv_low, w_qkv, preferred_element_type=jnp.float32
    )
    input_share = lax.psum_scatter(
        partial_input.astype(jnp.bfloat16), "tensor", scatter_dimension=0, tiled=True
    ).astype(jnp.float32)
    input_grad = (input_share + own_mixed_one).astype(jnp.bfloat16)
    bias_grads, up_bias_grad = lax.psum(
        (jnp.stack([qkv_bias_sums[0], qkv_bias_sums[2]]), up_bias_sum), "dp"
    )
    small_stack = jnp.stack(
        [
            sum_mixed_one,
            grad_gain_one,
            grad_bias_one,
            jnp.sum(grad_mixed_two, axis=0),
            grad_gain_two,
            grad_bias_two,
        ],
        axis=1,
    )
    qkv_share, out_share, small_share, up_share, down_share = (
        lax.psum_scatter(grad_qkv_t, "dp", scatter_dimension=0, tiled=True),
        lax.psum_scatter(grad_out_t, "dp", scatter_dimension=0, tiled=True),
        lax.psum_scatter(small_stack, "dp", scatter_dimension=0, tiled=True),
        lax.psum_scatter(grad_up_local, "dp", scatter_dimension=0, tiled=True),
        lax.psum_scatter(grad_down_t, "dp", scatter_dimension=0, tiled=True),
    )
    return (
        layer_out,
        input_grad,
        jnp.transpose(qkv_share, (1, 0, 2)),
        bias_grads,
        out_share.T,
        small_share[:, 0],
        small_share[:, 1],
        small_share[:, 2],
        up_share,
        up_bias_grad,
        down_share.T,
        small_share[:, 3],
        small_share[:, 4],
        small_share[:, 5],
    )


def solution(mesh):
    return jax.shard_map(
        per_device,
        mesh=mesh,
        in_specs=(
            P("dp", None),
            P("dp", None),
            P(None, None, "tensor"),
            P(None, "tensor"),
            P("tensor", None),
            P(),
            P(),
            P(),
            P(None, "tensor"),
            P("tensor"),
            P("tensor", None),
            P(),
            P(),
            P(),
            P("dp", None),
        ),
        out_specs=(
            P(("dp", "tensor"), None),
            P(("dp", "tensor"), None),
            P(None, "dp", "tensor"),
            P(None, "tensor"),
            P("tensor", "dp"),
            P("dp"),
            P("dp"),
            P("dp"),
            P("dp", "tensor"),
            P("tensor"),
            P("tensor", "dp"),
            P("dp"),
            P("dp"),
            P("dp"),
        ),
        check_vma=False,
    )
```

profile of v0, /device:TPU:0, one launch (start us, length us, event | category | flops | bytes accessed | tf_op | source)
XLA Modules:
  0.0 893.2 jit_solution(6782802428937616471)
XLA Ops:
  9.8 4.2 fusion.30
  15.4 51.2 %while.24 = (s32[]{:T(128)}, bf16[4,512,192]{1,2,0:T(8,128)(2,1)}, f32[4,3,512]{2,1,0:T(4,128)}, s32[4]{0:T(128)S(1)}, bf16[2,3072,192]{1,2,0:T(8,128)(2,1)S(1)}...) while((s32[]{:T(128)}, bf16[4,512,192]{1,2,0:T(8,128)(2,1)}, ...), condition=%wide.region_5.6_spmd, body=%wide.region_2.5_spmd.sunk | while | flops 630815232 | bytes 37824776 | solution.py:97
  19.3 2.0 fusion.103
  21.3 2.8 exponential_reduce_fusion.2
  24.8 2.7 fusion.104
  32.1 2.0 fusion.103
  34.1 2.8 exponential_reduce_fusion.2
  37.6 2.7 fusion.104
  44.9 2.0 fusion.103
  46.9 2.8 exponential_reduce_fusion.2
  50.4 2.7 fusion.104
  57.7 2.0 fusion.103
  59.7 2.8 exponential_reduce_fusion.2
  63.2 2.7 fusion.104
  68.7 3.7 convolution_convert_fusion.2
  77.5 118.8 %all-reduce.7.cloned.1.call-done = bf16[2048,768]{1,0:T(8,128)(2,1)} async-done(((bf16[2048,768]{1,0:T(8,128)(2,1)}), bf16[2048,768]{1,0:T(8,128)(2,1)}) %all-reduce.7.cloned.1.call-update) | async-done | bytes 3145744 | tf_op jit(solution)/shard_map/psum | solution.py:99
  196.3 4.1 fusion.23
  202.8 18.6 %multiply_convert_fusion.1 = (bf16[2048,768]{1,0:T(8,128)(2,1)S(1)}, f32[2048,768]{1,0:T(8,128)}, f32[2048,768]{1,0:T(8,128)}) fusion(f32[768]{0:T(1024)S(1)} %copy-done.42, bf16[768,768]{1,0:T(8,128)(2,1)S(1)} %copy-done, f32[768]{0:T(1024)S(1)} %copy-done.38, f32[768]{0:T(1024)S(1)} %copy-done.34, f32[2048]{0:T(1024)S(1)} %add_rsqrt_fusion.1, ...), kind=kOutput, calls=%fused_computation.53 | convolution fusion | flops 2533883904 | bytes 23228416 | tf_op jit(solution)/shard_map/dot_general | solution.py:108
  223.1 4.0 convolution_convert_fusion.1
  229.9 117.4 %all-reduce.9.cloned.1.call-done = bf16[2048,768]{1,0:T(8,128)(2,1)} async-done(((bf16[2048,768]{1,0:T(8,128)(2,1)}), bf16[2048,768]{1,0:T(8,128)(2,1)}) %all-reduce.9.cloned.1.call-update) | async-done | bytes 3145744 | tf_op jit(solution)/shard_map/psum | solution.py:112
  347.3 6.5 fusion.48
  353.9 3.9 multiply_reduce_fusion.3
  357.8 6.5 fusion.16
  367.0 10.4 %convert_reduce_fusion.1 = (f32[768]{0:T(1024)}, bf16[2048,768]{1,0:T(8,128)(2,1)S(1)}) fusion(f32[2048,768]{1,0:T(8,128)} %get-tuple-element.223, bf16[768,768]{1,0:T(8,128)(2,1)S(1)} %copy-done.45, f32[2048,768]{1,0:T(8,128)S(1)} %fusion.13, f32[2048,768]{1,0:T(8,128)} %get-tuple-element.242, f32[768]{0:T(1024)S(1)} %copy-done.43), kind=kOutput, calls=%fused_computation.45 | convolution fusion | flops 2444229888 | bytes 23205888 | tf_op jit(solution)/shard_map/td,fd->tf/dot_general | solution.py:130
  379.0 4.0 convolution_convert_fusion
  384.7 118.6 %all-reduce.11.cloned.1.call-done = bf16[2048,768]{1,0:T(8,128)(2,1)} async-done(((bf16[2048,768]{1,0:T(8,128)(2,1)}), bf16[2048,768]{1,0:T(8,128)(2,1)}) %all-reduce.11.cloned.1.call-update) | async-done | bytes 3145744 | tf_op jit(solution)/shard_map/psum | solution.py:139
  503.3 7.9 multiply_reduce_fusion.1
  511.6 5.7 fusion.52
  517.3 2.7 copy-done.11
  523.0 4.8 convolution_convert_fusion.3
  528.2 2.8 broadcast_in_dim.42
  531.0 148.0 %while.25 = (s32[]{:T(128)}, f32[2,3072,192]{1,2,0:T(8,128)}, bf16[4,512,192]{1,2,0:T(8,128)(2,1)}, s32[4]{0:T(128)S(1)}, bf16[3,2048,192]{1,2,0:T(8,128)(2,1)},...) while((s32[]{:T(128)}, f32[2,3072,192]{1,2,0:T(8,128)}, ...), condition=%wide.region_19.20_spmd, body=%wide.region_17.19_spmd.sunk | while | flops 1533639168 | bytes 149576176 | solution.py:191
  539.3 2.5 subtract_exponential_fusion.2
  542.7 5.6 multiply_reduce_fusion.7
  548.3 9.4 %multiply_convert_fusion.3 = bf16[3,512,1536]{2,1,0:T(8,128)(2,1)} fusion(f32[3,512,1536]{2,1,0:T(8,128)} %copy-done.2, f32[3,512,1536]{2,1,0:T(8,128)} %get-tuple-element.375, f32[3,512]{1,0:T(4,128)S(1)} %get-tuple-element.376), kind=kLoop, calls=%fused_computation.16.clone.1 | loop fusion | flops 7077888 | bytes 23599104 | tf_op jit(solution)/shard_map/while/body/eval_jaxpr/convert_element_type | solution.py:169
  557.8 4.2 convolution_multiply_fusion.5
  564.5 3.5 fusion.116
  576.4 2.5 subtract_exponential_fusion.2
  579.8 5.6 multiply_reduce_fusion.7
  585.4 9.5 %multiply_convert_fusion.3 = bf16[3,512,1536]{2,1,0:T(8,128)(2,1)} fusion(f32[3,512,1536]{2,1,0:T(8,128)} %copy-done.2, f32[3,512,1536]{2,1,0:T(8,128)} %get-tuple-element.375, f32[3,512]{1,0:T(4,128)S(1)} %get-tuple-element.376), kind=kLoop, calls=%fused_computation.16.clone.1 | loop fusion | flops 7077888 | bytes 23599104 | tf_op jit(solution)/shard_map/while/body/eval_jaxpr/convert_element_type | solution.py:169
  594.9 4.2 convolution_multiply_fusion.5
  601.7 3.5 fusion.116
  613.5 2.5 subtract_exponential_fusion.2
  616.9 5.5 multiply_reduce_fusion.7
  622.4 9.4 %multiply_convert_fusion.3 = bf16[3,512,1536]{2,1,0:T(8,128)(2,1)} fusion(f32[3,512,1536]{2,1,0:T(8,128)} %copy-done.2, f32[3,512,1536]{2,1,0:T(8,128)} %get-tuple-element.375, f32[3,512]{1,0:T(4,128)S(1)} %get-tuple-element.376), kind=kLoop, calls=%fused_computation.16.clone.1 | loop fusion | flops 7077888 | bytes 23599104 | tf_op jit(solution)/shard_map/while/body/eval_jaxpr/convert_element_type | solution.py:169
  631.8 4.2 convolution_multiply_fusion.5
  638.6 3.5 fusion.116
  650.4 2.5 subtract_exponential_fusion.2
  653.8 5.5 multiply_reduce_fusion.7
  659.4 9.4 %multiply_convert_fusion.3 = bf16[3,512,1536]{2,1,0:T(8,128)(2,1)} fusion(f32[3,512,1536]{2,1,0:T(8,128)} %copy-done.2, f32[3,512,1536]{2,1,0:T(8,128)} %get-tuple-element.375, f32[3,512]{1,0:T(4,128)S(1)} %get-tuple-element.376), kind=kLoop, calls=%fused_computation.16.clone.1 | loop fusion | flops 7077888 | bytes 23599104 | tf_op jit(solution)/shard_map/while/body/eval_jaxpr/convert_element_type | solution.py:169
  668.8 4.2 convolution_multiply_fusion.5
  675.5 3.5 fusion.116
  681.3 2.1 slice.88
  683.5 5.2 fusion.24
  688.6 2.8 copy.48
  691.8 4.0 bitcast_convert_fusion
  696.0 8.2 fusion.38
  704.3 8.6 fusion.44
  713.6 2.4 fusion.34
  716.4 14.7 %all-reduce.2 = (f32[2,192]{1,0:T(2,128)}, f32[768]{0:T(1024)}) all-reduce(f32[2,192]{1,0:T(2,128)S(1)} %pad_maximum_fusion.3, f32[768]{0:T(1024)S(1)} %copy-done.41), channel_id=1, replica_groups=mesh['dp'=8,'tensor'=4] {'dp'}, use_global_device_ids=true, to_apply=%region_23.24 | all-reduce | flops 1152 | bytes 9216 | tf_op jit(solution)/shard_map/psum | solution.py:207
  739.4 54.3 %reduce-scatter.11.cloned.1.call-done = bf16[512,768]{1,0:T(8,128)(2,1)} async-done(((bf16[2048,768]{1,0:T(8,128)(2,1)}), bf16[512,768]{1,0:T(8,128)(2,1)}) %reduce-scatter.11.cloned.1.call-update) | async-done | bytes 786448 | tf_op jit(solution)/shard_map/reduce_scatter | solution.py:203
  793.7 2.6 add_convert_fusion.2
  796.3 43.5 %reduce-scatter.17.cloned.1.call-done = f32[96,768]{1,0:T(8,128)} async-done(((f32[768,768]{1,0:T(8,128)}), f32[96,768]{1,0:T(8,128)}) %reduce-scatter.17.cloned.1.call-update) | async-done | bytes 294928 | tf_op jit(solution)/shard_map/reduce_scatter | solution.py:226
  839.9 46.3 %reduce-scatter.15.cloned.1.call-done = f32[96,768]{1,0:T(8,128)} async-done(((f32[768,768]{1,0:T(8,128)}), f32[96,768]{1,0:T(8,128)}) %reduce-scatter.15.cloned.1.call-update) | async-done | bytes 294928 | tf_op jit(solution)/shard_map/reduce_scatter | solution.py:225
  (290 shorter events, 94.7 us)
Async XLA Ops:
  7.2 195.6 %copy-start = (bf16[768,768]{1,0:T(8,128)(2,1)S(1)}, bf16[768,768]{1,0:T(8,128)(2,1)}, u32[]{:S(2)}) copy-start(bf16[768,768]{1,0:T(8,128)(2,1)} %param.27) | copy-start | bytes 3538948
  7.2 189.1 %all-reduce.7.cloned.1.call-start = ((), (), s32[]{:S(2)}) async-start(), calls=%async_computation.6 | async-start | bytes 6291456 | tf_op jit(solution)/shard_map/psum | solution.py:99
  72.4 274.9 %all-reduce.9.cloned.1.call-start = ((), (), s32[]{:S(2)}) async-start(), calls=%async_computation.7 | async-start | bytes 6291456 | tf_op jit(solution)/shard_map/psum | solution.py:112
  73.6 437.6 %copy-start.33 = (f32[768]{0:T(1024)}, f32[768]{0:T(1024)S(1)}, u32[]{:S(2)}) copy-start(f32[768]{0:T(1024)S(1)} %convert_element_type.132) | copy-start | bytes 9220
  196.3 4.1 copy-start.4
  196.3 4.7 copy-start.7
  196.3 6.5 copy-start.34
  196.3 6.5 copy-start.38
  196.3 6.5 copy-start.42
  201.0 20.5 %copy-start.25 = (f32[2048]{0:T(1024)}, f32[2048]{0:T(1024)S(1)}, u32[]{:S(2)}) copy-start(f32[2048]{0:T(1024)S(1)} %broadcast_multiply_fusion.5) | copy-start | bytes 24580
  202.8 18.6 %copy-start.29 = (f32[2048]{0:T(1024)}, f32[2048]{0:T(1024)S(1)}, u32[]{:S(2)}) copy-start(f32[2048]{0:T(1024)S(1)} %add_rsqrt_fusion.1) | copy-start | bytes 24580
  202.8 20.2 %copy-start.44 = (bf16[768,768]{1,0:T(8,128)(2,1)S(1)}, bf16[768,768]{1,0:T(8,128)(2,1)}, u32[]{:S(2)}) copy-start(bf16[768,768]{1,0:T(8,128)(2,1)} %param.29) | copy-start | bytes 3538948
  227.1 276.2 %all-reduce.11.cloned.1.call-start = ((), (), s32[]{:S(2)}) async-start(), calls=%async_computation.8 | async-start | bytes 6291456 | tf_op jit(solution)/shard_map/psum | solution.py:139
  347.3 6.6 copy-start.5
  347.3 6.6 copy-start.8
  347.3 6.6 copy-start.15
  347.3 6.6 copy-start.26
  347.3 6.6 copy-start.30
  347.3 6.6 copy-start.35
  347.3 6.6 copy-start.39
  347.3 6.6 copy-start.40
  353.8 4.0 copy-start.17
  353.8 4.0 copy-start.37
  364.4 2.6 copy-start.14
  364.4 2.6 copy-start.43
  364.4 2.6 copy-start.45
  367.0 10.4 %copy-start.10 = (f32[2048,768]{1,0:T(8,128)}, f32[2048,768]{1,0:T(8,128)S(1)}, u32[]{:S(2)}) copy-start(f32[2048,768]{1,0:T(8,128)S(1)} %fusion.13) | copy-start | bytes 18874372
  377.4 1.6 copy-start.47
  383.1 348.0 %reduce-scatter.21.cloned.1.call-start = ((), (), s32[]{:S(2)}) async-start(), calls=%async_computation.14 | async-start | bytes 442368
  384.7 126.5 %copy-start.27 = (f32[2048]{0:T(1024)S(1)}, f32[2048]{0:T(1024)}, u32[]{:S(2)}) copy-start(f32[2048]{0:T(1024)} %copy-done.25) | copy-start | bytes 24580
  384.7 126.5 %copy-start.31 = (f32[2048]{0:T(1024)S(1)}, f32[2048]{0:T(1024)}, u32[]{:S(2)}) copy-start(f32[2048]{0:T(1024)} %copy-done.29) | copy-start | bytes 24580
  384.7 126.5 %copy-start.36 = (f32[768]{0:T(1024)S(1)}, f32[768]{0:T(1024)}, u32[]{:S(2)}) copy-start(f32[768]{0:T(1024)} %convert_element_type.133) | copy-start | bytes 9220
  503.3 8.0 copy-start.6
  503.3 8.0 copy-start.9
  503.3 8.3 copy-start.18
  511.6 8.4 copy-start.20
  517.3 2.7 copy-start.11
  517.3 5.7 copy-start.22
  523.0 212.8 %reduce-scatter.13.cloned.1.call-start = ((), (), s32[]{:S(2)}) async-start(), calls=%async_computation.10 | async-start | bytes 884736 | tf_op jit(solution)/shard_map/reduce_scatter | solution.py:223
  527.9 209.6 %reduce-scatter.19.cloned.1.call-start = ((), (), s32[]{:S(2)}) async-start(), calls=%async_computation.13 | async-start | bytes 2211840
  531.0 10.8 %copy-start.23 = (s32[3072]{0:T(1024)}, s32[3072]{0:T(1024)S(1)}, u32[]{:S(2)}) copy-start(s32[3072]{0:T(1024)S(1)} %get-tuple-element.459) | copy-start | bytes 36868 | tf_op jit(solution)/shard_map/while
  541.8 6.5 copy-start.2
  557.8 4.2 copy-start.3
  562.0 6.1 copy-start.24
  568.0 10.8 %copy-start.23 = (s32[3072]{0:T(1024)}, s32[3072]{0:T(1024)S(1)}, u32[]{:S(2)}) copy-start(s32[3072]{0:T(1024)S(1)} %get-tuple-element.459) | copy-start | bytes 36868 | tf_op jit(solution)/shard_map/while
  578.9 6.6 copy-start.2
  594.9 4.2 copy-start.3
  599.1 6.0 copy-start.24
  605.1 10.8 %copy-start.23 = (s32[3072]{0:T(1024)}, s32[3072]{0:T(1024)S(1)}, u32[]{:S(2)}) copy-start(s32[3072]{0:T(1024)S(1)} %get-tuple-element.459) | copy-start | bytes 36868 | tf_op jit(solution)/shard_map/while
  615.9 6.5 copy-start.2
  631.8 4.2 copy-start.3
  636.0 6.0 copy-start.24
  642.1 10.8 %copy-start.23 = (s32[3072]{0:T(1024)}, s32[3072]{0:T(1024)S(1)}, u32[]{:S(2)}) copy-start(s32[3072]{0:T(1024)S(1)} %get-tuple-element.459) | copy-start | bytes 36868 | tf_op jit(solution)/shard_map/while
  652.9 6.5 copy-start.2
  668.8 4.2 copy-start.3
  673.0 6.0 copy-start.24
  683.4 8.4 copy-start.46
  691.5 102.2 %reduce-scatter.11.cloned.1.call-start = ((), (), s32[]{:S(2)}) async-start(), calls=%async_computation.9 | async-start | bytes 3932160 | tf_op jit(solution)/shard_map/reduce_scatter | solution.py:203
  695.9 8.4 copy-start.28
  695.9 8.4 copy-start.32
  695.9 144.0 %reduce-scatter.17.cloned.1.call-start = ((), (), s32[]{:S(2)}) async-start(), calls=%async_computation.12 | async-start | bytes 2654208 | tf_op jit(solution)/shard_map/reduce_scatter | solution.py:226
  704.2 182.0 %reduce-scatter.15.cloned.1.call-start = ((), (), s32[]{:S(2)}) async-start(), calls=%async_computation.11 | async-start | bytes 2654208 | tf_op jit(solution)/shard_map/reduce_scatter | solution.py:225
  704.3 181.9 %copy-start.1 = (bf16[768,768]{1,0:T(8,128)(2,1)S(1)}, bf16[768,768]{1,0:T(8,128)(2,1)}, u32[]{:S(2)}) copy-start(bf16[768,768]{1,0:T(8,128)(2,1)} %param.27) | copy-start | bytes 3538948
  712.9 3.6 copy-start.41
  (11 other events, 9.9 us)
Sparse Core Ops, SparseCore 0:
  72.5 123.7 all-reduce.6
  227.2 120.0 all-reduce.8
  383.2 120.0 all-reduce.10
  523.1 32.8 reduce-scatter.20
  559.0 34.9 reduce-scatter.12
  691.6 39.2 reduce-scatter.18
  733.2 60.4 reduce-scatter.10
  797.6 42.2 reduce-scatter.16
  843.8 42.3 reduce-scatter.14
where the time goes:
time: 902 us; the launch traced here: 893 us
  waiting for transfers between devices  499 us (55%)
  matrix products  156 us (17%)
  other arithmetic  122 us (14%)
  local copies, waits for them, and re-layouts  70.1 us (8%)
  between operations  15 us (2%)
  blocking collectives  14.7 us (2%)
  loops' own time  13.6 us (2%)
    psum x1, waiting for transfers between devices, per_device(): lax.psum(jnp.dot(context, w_out, preferred_element_type=jnp.float32).asty...  119 us
    psum x1, waiting for transfers between devices, per_device(): lax.psum(partial_hidden.astype(jnp.bfloat16), 'tensor').astype(jnp.float32)  119 us
    psum x1, waiting for transfers between devices, per_device(): lax.psum(jnp.dot(activated, w_down, preferred_element_type=jnp.float32).a...  117 us
    reduce_scatter x1, waiting for transfers between devices, per_device(): lax.psum_scatter(partial_input.astype(jnp.bfloat16), 'tensor', scatter_di...  54.3 us
    reduce_scatter x1, waiting for transfers between devices, per_device(): lax.psum_scatter(grad_up_local, 'dp', scatter_dimension=0, tiled=True)  46.3 us
    reduce_scatter x1, waiting for transfers between devices, per_device(): lax.psum_scatter(grad_down_t, 'dp', scatter_dimension=0, tiled=True)  43.5 us
    convert_element_type x4, other arithmetic, backward_block(): (soft_weights * (grad_weights - row_shift)).astype(jnp.bfloat16)  37.7 us
    dot_general x4, matrix products, backward_block(): jnp.einsum('qhd,khd->hqk', upstream_block, window[1], preferred_element_t...  22.2 us
  transfers between devices with their start and end apart: 9, of which 6 were waited for; matrix products, arithmetic and copies ran while one was open for 22% of the time, Pallas kernels for 0%

commit v1 on v0

--- a/solution.py
+++ b/solution.py
@@ -96,9 +96,14 @@
 
     contexts, log_totals = lax.map(forward_block, jnp.arange(blocks, dtype=jnp.int32))
     context = contexts.reshape(rows, local_width)
-    attended = lax.psum(
-        jnp.dot(context, w_out, preferred_element_type=jnp.float32).astype(jnp.bfloat16), "tensor"
-    ).astype(jnp.float32)
+    attended = (
+        lax.all_gather(
+            jnp.dot(context, w_out, preferred_element_type=jnp.float32).astype(jnp.bfloat16),
+            "tensor",
+        )
+        .sum(axis=0)
+        .astype(jnp.float32)
+    )
     mixed_one = tokens.astype(jnp.float32) + attended + b_out.astype(jnp.float32)
     gain_one = ln1_gain.astype(jnp.float32)
     hidden_one, normed_one, spread_one = norm_forward(

time: 902 us -> 1010 us (1.12)
  waiting for transfers between devices: 499 us -> 596 us
    all_gather x0 -> x1, waiting for transfers between devices: none -> 216 us  [per_device(): lax.all_gather(jnp.dot(context, w_out, preferred_element_type=jnp.float32...]
    psum x1 -> x0, waiting for transfers between devices: 119 us -> none  [per_device(): lax.psum(jnp.dot(context, w_out, preferred_element_type=jnp.float32).asty...]
  transfers between devices with their start and end apart: 9 -> 9, of which waited for: 6 -> 6; matrix products, arithmetic and copies ran while one was open for 22% -> 20% of each run, Pallas kernels for 0% -> 0%
where the time goes in v1:
time: 1010 us; the launch traced here: 998 us
  waiting for transfers between devices  596 us (59%)
  matrix products  156 us (15%)
  other arithmetic  131 us (13%)
  local copies, waits for them, and re-layouts  70.9 us (7%)
  blocking collectives  14.6 us (1%)
  between operations  14.6 us (1%)
  loops' own time  13.6 us (1%)
    all_gather x1, waiting for transfers between devices, per_device(): lax.all_gather(jnp.dot(context, w_out, preferred_element_type=jnp.float32...  216 us
    psum x1, waiting for transfers between devices, per_device(): lax.psum(partial_hidden.astype(jnp.bfloat16), 'tensor').astype(jnp.float32)  119 us
    psum x1, waiting for transfers between devices, per_device(): lax.psum(jnp.dot(activated, w_down, preferred_element_type=jnp.float32).a...  117 us
    reduce_scatter x1, waiting for transfers between devices, per_device(): lax.psum_scatter(partial_input.astype(jnp.bfloat16), 'tensor', scatter_di...  54.5 us
    reduce_scatter x1, waiting for transfers between devices, per_device(): lax.psum_scatter(grad_up_local, 'dp', scatter_dimension=0, tiled=True)  46.3 us
    reduce_scatter x1, waiting for transfers between devices, per_device(): lax.psum_scatter(grad_down_t, 'dp', scatter_dimension=0, tiled=True)  43.6 us
    convert_element_type x4, other arithmetic, backward_block(): (soft_weights * (grad_weights - row_shift)).astype(jnp.bfloat16)  37.7 us
    dot_general x4, matrix products, backward_block(): jnp.einsum('qhd,khd->hqk', upstream_block, window[1], preferred_element_t...  22.2 us
  transfers between devices with their start and end apart: 9, of which 6 were waited for; matrix products, arithmetic and copies ran while one was open for 20% of the time, Pallas kernels for 0%

profile of v1, /device:TPU:0, one launch (start us, length us, event | category | flops | bytes accessed | tf_op | source)
XLA Modules:
  0.0 998.3 jit_solution(14041933590947355672)
XLA Ops:
  9.8 4.2 fusion.30
  15.4 51.2 %while.24 = (s32[]{:T(128)}, bf16[4,512,192]{1,2,0:T(8,128)(2,1)}, f32[4,3,512]{2,1,0:T(4,128)}, s32[4]{0:T(128)S(1)}, bf16[2,3072,192]{1,2,0:T(8,128)(2,1)S(1)}...) while((s32[]{:T(128)}, bf16[4,512,192]{1,2,0:T(8,128)(2,1)}, ...), condition=%wide.region_5.6_spmd, body=%wide.region_2.5_spmd.sunk | while | flops 630815232 | bytes 37824776 | solution.py:97
  19.3 2.0 fusion.103
  21.3 2.8 exponential_reduce_fusion.2
  24.8 2.7 fusion.104
  32.1 2.0 fusion.103
  34.1 2.8 exponential_reduce_fusion.2
  37.6 2.7 fusion.104
  44.9 2.0 fusion.103
  46.9 2.8 exponential_reduce_fusion.2
  50.4 2.7 fusion.104
  59.7 2.8 exponential_reduce_fusion.2
  63.2 2.7 fusion.104
  68.7 3.7 convolution_convert_fusion.2
  77.1 216.3 %all-gather.3.cloned.1.call-done = bf16[8192,768]{1,0:T(8,128)(2,1)} async-done(((bf16[2048,768]{1,0:T(8,128)(2,1)}), bf16[8192,768]{1,0:T(8,128)(2,1)}) %all-gather.3.cloned.1.call-update) | async-done | bytes 12582928 | tf_op jit(solution)/shard_map/all_gather | solution.py:100
  293.4 8.9 reduce_sum.184
  302.4 4.1 fusion.23
  308.9 18.6 %multiply_convert_fusion.1 = (bf16[2048,768]{1,0:T(8,128)(2,1)S(1)}, f32[2048,768]{1,0:T(8,128)}, f32[2048,768]{1,0:T(8,128)}) fusion(f32[768]{0:T(1024)S(1)} %copy-done.42, bf16[768,768]{1,0:T(8,128)(2,1)S(1)} %copy-done, f32[768]{0:T(1024)S(1)} %copy-done.38, f32[768]{0:T(1024)S(1)} %copy-done.34, f32[2048]{0:T(1024)S(1)} %add_rsqrt_fusion.1, ...), kind=kOutput, calls=%fused_computation.53 | convolution fusion | flops 2533883904 | bytes 23228416 | tf_op jit(solution)/shard_map/dot_general | solution.py:113
  329.2 4.0 convolution_convert_fusion.1
  336.0 116.6 %all-reduce.6.cloned.1.call-done = bf16[2048,768]{1,0:T(8,128)(2,1)} async-done(((bf16[2048,768]{1,0:T(8,128)(2,1)}), bf16[2048,768]{1,0:T(8,128)(2,1)}) %all-reduce.6.cloned.1.call-update) | async-done | bytes 3145744 | tf_op jit(solution)/shard_map/psum | solution.py:117
  452.6 5.7 fusion.48
  459.1 3.9 multiply_reduce_fusion.3
  463.0 6.5 fusion.16
  472.2 10.4 %convert_reduce_fusion.1 = (f32[768]{0:T(1024)}, bf16[2048,768]{1,0:T(8,128)(2,1)S(1)}) fusion(f32[2048,768]{1,0:T(8,128)} %get-tuple-element.223, bf16[768,768]{1,0:T(8,128)(2,1)S(1)} %copy-done.45, f32[2048,768]{1,0:T(8,128)S(1)} %fusion.13, f32[2048,768]{1,0:T(8,128)} %get-tuple-element.242, f32[768]{0:T(1024)S(1)} %copy-done.43), kind=kOutput, calls=%fused_computation.45 | convolution fusion | flops 2444229888 | bytes 23205888 | tf_op jit(solution)/shard_map/td,fd->tf/dot_general | solution.py:135
  484.2 4.0 convolution_convert_fusion
  489.7 118.8 %all-reduce.8.cloned.1.call-done = bf16[2048,768]{1,0:T(8,128)(2,1)} async-done(((bf16[2048,768]{1,0:T(8,128)(2,1)}), bf16[2048,768]{1,0:T(8,128)(2,1)}) %all-reduce.8.cloned.1.call-update) | async-done | bytes 3145744 | tf_op jit(solution)/shard_map/psum | solution.py:144
  608.4 7.9 multiply_reduce_fusion.1
  616.8 5.7 fusion.52
  622.5 2.7 copy-done.11
  628.2 4.8 convolution_convert_fusion.3
  633.5 2.8 broadcast_in_dim.42
  636.3 148.0 %while.25 = (s32[]{:T(128)}, f32[2,3072,192]{1,2,0:T(8,128)}, bf16[4,512,192]{1,2,0:T(8,128)(2,1)}, s32[4]{0:T(128)S(1)}, bf16[3,2048,192]{1,2,0:T(8,128)(2,1)},...) while((s32[]{:T(128)}, f32[2,3072,192]{1,2,0:T(8,128)}, ...), condition=%wide.region_19.20_spmd, body=%wide.region_17.19_spmd.sunk | while | flops 1533639168 | bytes 149576176 | solution.py:196
  644.6 2.5 subtract_exponential_fusion.2
  648.1 5.6 multiply_reduce_fusion.7
  653.6 9.4 multiply_convert_fusion.3
  663.1 4.2 convolution_multiply_fusion.5
  669.9 3.5 fusion.116
  681.7 2.5 subtract_exponential_fusion.2
  685.1 5.6 multiply_reduce_fusion.7
  690.8 9.5 multiply_convert_fusion.3
  700.2 4.2 convolution_multiply_fusion.5
  707.0 3.5 fusion.116
  718.8 2.5 subtract_exponential_fusion.2
  722.2 5.5 multiply_reduce_fusion.7
  727.8 9.4 multiply_convert_fusion.3
  737.2 4.2 convolution_multiply_fusion.5
  743.9 3.5 fusion.116
  755.7 2.5 subtract_exponential_fusion.2
  759.2 5.5 multiply_reduce_fusion.7
  764.7 9.4 multiply_convert_fusion.3
  774.1 4.2 convolution_multiply_fusion.5
  780.9 3.5 fusion.116
  786.7 2.1 slice.88
  788.8 5.2 fusion.24
  794.0 2.8 copy.48
  797.0 4.0 bitcast_convert_fusion
  801.2 8.2 fusion.38
  809.5 8.6 fusion.44
  818.8 2.4 fusion.34
  821.6 14.6 %all-reduce.2 = (f32[2,192]{1,0:T(2,128)}, f32[768]{0:T(1024)}) all-reduce(f32[2,192]{1,0:T(2,128)S(1)} %pad_maximum_fusion.3, f32[768]{0:T(1024)S(1)} %copy-done.41), channel_id=1, replica_groups=mesh['dp'=8,'tensor'=4] {'dp'}, use_global_device_ids=true, to_apply=%region_23.24 | all-reduce | flops 1152 | bytes 9216 | tf_op jit(solution)/shard_map/psum | solution.py:212
  844.6 54.5 %reduce-scatter.11.cloned.1.call-done = bf16[512,768]{1,0:T(8,128)(2,1)} async-done(((bf16[2048,768]{1,0:T(8,128)(2,1)}), bf16[512,768]{1,0:T(8,128)(2,1)}) %reduce-scatter.11.cloned.1.call-update) | async-done | bytes 786448 | tf_op jit(solution)/shard_map/reduce_scatter | solution.py:208
  899.0 2.6 add_convert_fusion.2
  901.7 43.6 %reduce-scatter.17.cloned.1.call-done = f32[96,768]{1,0:T(8,128)} async-done(((f32[768,768]{1,0:T(8,128)}), f32[96,768]{1,0:T(8,128)}) %reduce-scatter.17.cloned.1.call-update) | async-done | bytes 294928 | tf_op jit(solution)/shard_map/reduce_scatter | solution.py:231
  945.2 46.3 %reduce-scatter.15.cloned.1.call-done = f32[96,768]{1,0:T(8,128)} async-done(((f32[768,768]{1,0:T(8,128)}), f32[96,768]{1,0:T(8,128)}) %reduce-scatter.15.cloned.1.call-update) | async-done | bytes 294928 | tf_op jit(solution)/shard_map/reduce_scatter | solution.py:230
  (291 shorter events, 96.9 us)
Async XLA Ops:
  7.2 301.7 %copy-start = (bf16[768,768]{1,0:T(8,128)(2,1)S(1)}, bf16[768,768]{1,0:T(8,128)(2,1)}, u32[]{:S(2)}) copy-start(bf16[768,768]{1,0:T(8,128)(2,1)} %param.27) | copy-start | bytes 3538948
  7.2 286.2 %all-gather.3.cloned.1.call-start = ((), (), s32[]{:S(2)}) async-start(), calls=%async_computation.12 | async-start | bytes 15728640 | tf_op jit(solution)/shard_map/all_gather | solution.py:100
  72.4 380.2 %all-reduce.6.cloned.1.call-start = ((), (), s32[]{:S(2)}) async-start(), calls=%async_computation.6 | async-start | bytes 6291456 | tf_op jit(solution)/shard_map/psum | solution.py:117
  73.3 543.1 %copy-start.33 = (f32[768]{0:T(1024)}, f32[768]{0:T(1024)S(1)}, u32[]{:S(2)}) copy-start(f32[768]{0:T(1024)S(1)} %convert_element_type.134) | copy-start | bytes 9220
  302.4 4.1 copy-start.4
  302.4 4.7 copy-start.7
  302.4 6.5 copy-start.34
  302.4 6.5 copy-start.38
  302.4 6.5 copy-start.42
  307.1 20.5 %copy-start.25 = (f32[2048]{0:T(1024)}, f32[2048]{0:T(1024)S(1)}, u32[]{:S(2)}) copy-start(f32[2048]{0:T(1024)S(1)} %broadcast_multiply_fusion.5) | copy-start | bytes 24580
  308.9 18.6 %copy-start.29 = (f32[2048]{0:T(1024)}, f32[2048]{0:T(1024)S(1)}, u32[]{:S(2)}) copy-start(f32[2048]{0:T(1024)S(1)} %add_rsqrt_fusion.1) | copy-start | bytes 24580
  308.9 20.2 %copy-start.44 = (bf16[768,768]{1,0:T(8,128)(2,1)S(1)}, bf16[768,768]{1,0:T(8,128)(2,1)}, u32[]{:S(2)}) copy-start(bf16[768,768]{1,0:T(8,128)(2,1)} %param.29) | copy-start | bytes 3538948
  333.2 275.3 %all-reduce.8.cloned.1.call-start = ((), (), s32[]{:S(2)}) async-start(), calls=%async_computation.7 | async-start | bytes 6291456 | tf_op jit(solution)/shard_map/psum | solution.py:144
  452.5 5.8 copy-start.5
  452.6 5.8 copy-start.8
  452.6 6.5 copy-start.15
  452.6 6.5 copy-start.26
  452.6 6.5 copy-start.30
  452.6 6.5 copy-start.35
  452.6 6.5 copy-start.39
  452.6 6.5 copy-start.40
  458.3 4.7 copy-start.17
  458.3 4.7 copy-start.37
  469.6 2.6 copy-start.14
  469.6 2.6 copy-start.43
  469.6 2.6 copy-start.45
  472.2 10.4 %copy-start.10 = (f32[2048,768]{1,0:T(8,128)}, f32[2048,768]{1,0:T(8,128)S(1)}, u32[]{:S(2)}) copy-start(f32[2048,768]{1,0:T(8,128)S(1)} %fusion.13) | copy-start | bytes 18874372
  482.5 1.6 copy-start.47
  488.2 348.0 %reduce-scatter.21.cloned.1.call-start = ((), (), s32[]{:S(2)}) async-start(), calls=%async_computation.14 | async-start | bytes 442368
  489.7 126.7 %copy-start.27 = (f32[2048]{0:T(1024)S(1)}, f32[2048]{0:T(1024)}, u32[]{:S(2)}) copy-start(f32[2048]{0:T(1024)} %copy-done.25) | copy-start | bytes 24580
  489.7 126.7 %copy-start.31 = (f32[2048]{0:T(1024)S(1)}, f32[2048]{0:T(1024)}, u32[]{:S(2)}) copy-start(f32[2048]{0:T(1024)} %copy-done.29) | copy-start | bytes 24580
  489.7 126.8 %copy-start.36 = (f32[768]{0:T(1024)S(1)}, f32[768]{0:T(1024)}, u32[]{:S(2)}) copy-start(f32[768]{0:T(1024)} %convert_element_type.135) | copy-start | bytes 9220
  608.4 8.0 copy-start.6
  608.4 8.0 copy-start.9
  608.4 8.3 copy-start.18
  616.8 8.4 copy-start.20
  622.5 2.7 copy-start.11
  622.5 5.7 copy-start.22
  628.1 212.8 %reduce-scatter.13.cloned.1.call-start = ((), (), s32[]{:S(2)}) async-start(), calls=%async_computation.9 | async-start | bytes 884736 | tf_op jit(solution)/shard_map/reduce_scatter | solution.py:228
  633.1 209.5 %reduce-scatter.19.cloned.1.call-start = ((), (), s32[]{:S(2)}) async-start(), calls=%async_computation.13 | async-start | bytes 2211840
  636.3 10.8 %copy-start.23 = (s32[3072]{0:T(1024)}, s32[3072]{0:T(1024)S(1)}, u32[]{:S(2)}) copy-start(s32[3072]{0:T(1024)S(1)} %get-tuple-element.459) | copy-start | bytes 36868 | tf_op jit(solution)/shard_map/while
  647.1 6.5 copy-start.2
  663.1 4.2 copy-start.3
  667.3 6.1 copy-start.24
  673.4 10.8 %copy-start.23 = (s32[3072]{0:T(1024)}, s32[3072]{0:T(1024)S(1)}, u32[]{:S(2)}) copy-start(s32[3072]{0:T(1024)S(1)} %get-tuple-element.459) | copy-start | bytes 36868 | tf_op jit(solution)/shard_map/while
  684.2 6.6 copy-start.2
  700.2 4.2 copy-start.3
  704.4 6.0 copy-start.24
  710.5 10.8 %copy-start.23 = (s32[3072]{0:T(1024)}, s32[3072]{0:T(1024)S(1)}, u32[]{:S(2)}) copy-start(s32[3072]{0:T(1024)S(1)} %get-tuple-element.459) | copy-start | bytes 36868 | tf_op jit(solution)/shard_map/while
  721.3 6.5 copy-start.2
  737.2 4.2 copy-start.3
  741.4 6.0 copy-start.24
  747.4 10.8 %copy-start.23 = (s32[3072]{0:T(1024)}, s32[3072]{0:T(1024)S(1)}, u32[]{:S(2)}) copy-start(s32[3072]{0:T(1024)S(1)} %get-tuple-element.459) | copy-start | bytes 36868 | tf_op jit(solution)/shard_map/while
  758.2 6.5 copy-start.2
  774.1 4.2 copy-start.3
  778.3 6.0 copy-start.24
  788.8 8.2 copy-start.46
  796.8 102.2 %reduce-scatter.11.cloned.1.call-start = ((), (), s32[]{:S(2)}) async-start(), calls=%async_computation.8 | async-start | bytes 3932160 | tf_op jit(solution)/shard_map/reduce_scatter | solution.py:208
  801.1 8.3 copy-start.28
  801.1 8.3 copy-start.32
  801.1 144.1 %reduce-scatter.17.cloned.1.call-start = ((), (), s32[]{:S(2)}) async-start(), calls=%async_computation.11 | async-start | bytes 2654208 | tf_op jit(solution)/shard_map/reduce_scatter | solution.py:231
  809.4 182.2 %reduce-scatter.15.cloned.1.call-start = ((), (), s32[]{:S(2)}) async-start(), calls=%async_computation.10 | async-start | bytes 2654208 | tf_op jit(solution)/shard_map/reduce_scatter | solution.py:230
  809.5 182.1 %copy-start.1 = (bf16[768,768]{1,0:T(8,128)(2,1)S(1)}, bf16[768,768]{1,0:T(8,128)(2,1)}, u32[]{:S(2)}) copy-start(bf16[768,768]{1,0:T(8,128)(2,1)} %param.27) | copy-start | bytes 3538948
  818.1 3.6 copy-start.41
  (11 other events, 9.9 us)
Sparse Core Ops, SparseCore 0:
  72.5 220.9 all-gather.2
  333.3 119.2 all-reduce.5
  488.4 120.0 all-reduce.7
  628.3 32.8 reduce-scatter.20
  664.2 34.9 reduce-scatter.12
  796.9 39.3 reduce-scatter.18
  838.6 60.4 reduce-scatter.10
  903.0 42.2 reduce-scatter.16
  949.2 42.3 reduce-scatter.14
